TPU v7x, 32 devices: a whole 2x2x4 slice. The times are simulated.
32 devices in a mesh: samp: 4 (over y, x), var: 8 (over z, core).
Axes of the slice: x: 2, y: 2, z: 4, core: 2. Of those that a mesh axis runs over, the one named last changes fastest.
Arguments:
- dosage: bfloat16 [8192, 16384], P('samp', 'var'), may hold values from -6 to 6
- traits: float32 [8192, 128], P(('samp', 'var')), may hold values from -6 to 6
- coef_now: float32 [128, 256, 128], P('var', 'samp'), may hold values from -6 to 6
- coef_prev: float32 [128, 256, 128], P('var', 'samp'), may hold values from -6 to 6
- block_inverse: bfloat16 [128, 256, 4, 256], P('var', 'samp'), may hold values from -0.1875 to 0.1875
- penalty: float32 [128], replicated, may hold values from 0.05 to 0.5
- block_start: int32 [64], replicated, may hold values from 0 to 1, as said below
- unit_owner: int32 [64], replicated, may hold values from 0 to 7, as said below
Outputs:
- coef_next: float32 [128, 256, 128], P('var', 'samp')
- residual: float32 [8192, 128], P(('samp', 'var'))
Inputs may be any that keep to these rules, and one draw needn't show every extreme that they name: `block_start`: 1 where a linkage block begins, else 0. The first unit of every device's 8 units begins a block, and a block holds 1 to 4 units of 256 variants. `unit_owner`: the index along var of the device that owns each unit's block, equal for all units of a block. For a unit of the device with index d along var it is (d + j) modulo the size of var, with 1 <= j <= 4. An owner holds at most 16 units and some owner holds exactly 16; the units of one device that belong to one owner are at most 4, and some device has exactly 4 for one owner.
All inputs are finite; a program needn't handle non-finite values.
Results may differ from a plain program's by a relative error of at most 0.0072.
Values may be sent and summed in bfloat16 or wider, within the bound.
No kernel may reach another device: no remote copies, remote signals or barrier semaphores. Data moves between devices by JAX's collectives and lax.ppermute only.
A program may use at most 64 MiB of HBM per device.

v0:
```python
import math
import jax
import jax.numpy as jnp
from jax import lax
from jax.sharding import PartitionSpec as P

MOMENTA = (0.4, 0.55)


def shifted(block, axis, distance):
    devices = range(lax.axis_size(axis))
    route = [((i - distance) % len(devices), i) for i in devices]
    return lax.ppermute(block, axis, route)


def unit_tables(block_start, unit_owner, per_device, owners):
    unit_count = block_start.shape[0]
    unit_ids = jnp.arange(unit_count, dtype=jnp.int32)
    shard_of = unit_ids // per_device
    owner_hot = (unit_owner[:, None] == jnp.arange(owners, dtype=jnp.int32)[None, :]).astype(
        jnp.int32
    )
    running = jnp.cumsum(owner_hot, axis=0) - owner_hot
    slot_index = jnp.sum(running * owner_hot, axis=1)
    first_unit = shard_of * per_device
    before_shard = jnp.sum(running[first_unit] * owner_hot, axis=1)
    pair_place = slot_index - before_shard
    block_begin = lax.cummax(jnp.where(block_start == 1, unit_ids, 0), axis=0)
    block_later = lax.cummin(
        jnp.where(block_start == 1, unit_ids, unit_count), axis=0, reverse=True
    )
    block_follow = jnp.concatenate([block_later[1:], jnp.full((1,), unit_count, jnp.int32)])
    block_length = block_follow - block_begin
    offset = unit_ids - block_begin
    return (shard_of, slot_index, pair_place, offset, block_length)


def shards(dosage, traits, coef_now, coef_prev, block_inverse, penalty, block_start, unit_owner):
    owners = lax.axis_size("var")
    quarters = lax.axis_size("samp")
    var_index = lax.axis_index("var")
    samp_index = lax.axis_index("samp")
    capacity = coef_now.shape[0]
    quarter_rows = coef_now.shape[1]
    right_cols = coef_now.shape[2]
    unit_rows = block_inverse.shape[3]
    block_most = block_inverse.shape[2]
    per_device = dosage.shape[1] // unit_rows
    pair_cap = min(block_most, per_device)
    reach = capacity // pair_cap
    samples = dosage.shape[0] * quarters
    variants = dosage.shape[1] * owners
    inv_scale = 1.0 / math.sqrt(variants)
    grad_scale = 0.5 / math.sqrt(samples)
    shard_of, slot_index, pair_place, offset, block_length = unit_tables(
        block_start, unit_owner, per_device, owners
    )
    owner_gap = (unit_owner - shard_of) % owners
    unit_code = (owner_gap - 1) * pair_cap + pair_place
    columns = jnp.arange(reach * pair_cap, dtype=jnp.int32)
    local_ids = var_index * per_device + jnp.arange(per_device, dtype=jnp.int32)
    local_code = unit_code[local_ids]
    matches = local_code[None, :] == columns[:, None]
    send_unit = jnp.sum(
        matches.astype(jnp.int32) * jnp.arange(per_device, dtype=jnp.int32)[None, :], axis=1
    )
    send_live = jnp.any(matches, axis=1)
    owned_flag = unit_owner == var_index
    slot_match = owned_flag[None, :] & (
        slot_index[None, :] == jnp.arange(capacity, dtype=jnp.int32)[:, None]
    )
    slot_hits = slot_match.astype(jnp.int32)
    slot_live = jnp.any(slot_match, axis=1)
    slot_code = jnp.sum(slot_hits * unit_code[None, :], axis=1)
    slot_offset = jnp.sum(slot_hits * offset[None, :], axis=1)
    slot_length = jnp.sum(slot_hits * block_length[None, :], axis=1)
    back_match = slot_live[None, :] & (slot_code[None, :] == columns[:, None])
    back_slot = jnp.sum(
        back_match.astype(jnp.int32) * jnp.arange(capacity, dtype=jnp.int32)[None, :], axis=1
    )
    back_live = jnp.any(back_match, axis=1)
    within = jnp.arange(block_most, dtype=jnp.int32)
    member_ids = jnp.clip(
        jnp.arange(capacity, dtype=jnp.int32)[:, None] - slot_offset[:, None] + within[None, :],
        0,
        capacity - 1,
    )
    member_live = (within[None, :] < slot_length[:, None]) & slot_live[:, None]
    panel_rows = block_inverse.reshape(capacity, quarter_rows, block_most * unit_rows)
    zero_half = jnp.zeros((), jnp.bfloat16)
    current, previous = (coef_now, coef_prev)
    residual = traits
    for momentum in MOMENTA:
        point = current + momentum * (current - previous)
        send_outgoing = jnp.where(
            back_live[:, None, None], point.astype(jnp.bfloat16)[back_slot], zero_half
        )
        send_outgoing = send_outgoing.reshape(reach, pair_cap, quarter_rows, right_cols)
        send_pieces = []
        for send_gap in range(1, reach + 1):
            send_pieces.append(shifted(send_outgoing[send_gap - 1], "var", -send_gap))
        send_received = jnp.stack(send_pieces).reshape(reach * pair_cap, quarter_rows, right_cols)
        local_rows = send_received[local_code]
        send_gathered = lax.all_gather(local_rows[:, None], "samp", axis=1, tiled=True)
        values = send_gathered.reshape(per_device * unit_rows, right_cols)
        summed = lax.psum_scatter(
            jnp.dot(dosage, values, preferred_element_type=jnp.float32) * inv_scale,
            "var",
            scatter_dimension=0,
            tiled=True,
        )
        residual = summed - traits
        residual_b = lax.all_gather(residual.astype(jnp.bfloat16), "var", axis=0, tiled=True)
        partial_grad = (
            lax.dot_general(
                dosage, residual_b, (((0,), (0,)), ((), ())), preferred_element_type=jnp.float32
            )
            * grad_scale
        )
        shaped = partial_grad.reshape(per_device, quarters, quarter_rows, right_cols)
        grad_sum = lax.psum(shaped, "samp")
        own_grad = lax.dynamic_index_in_dim(grad_sum, samp_index, 1, keepdims=False)
        outgoing = jnp.where(
            send_live[:, None, None], own_grad.astype(jnp.bfloat16)[send_unit], zero_half
        )
        outgoing = outgoing.reshape(reach, pair_cap, quarter_rows, right_cols)
        pieces = []
        for gap in range(1, reach + 1):
            pieces.append(shifted(outgoing[gap - 1], "var", gap))
        received = jnp.stack(pieces).reshape(reach * pair_cap, quarter_rows, right_cols)
        held_rows = jnp.where(slot_live[:, None, None], received[slot_code], zero_half)
        gathered = lax.all_gather(held_rows[:, None], "samp", axis=1, tiled=True)
        whole_grad = gathered.reshape(capacity, unit_rows, right_cols)
        block_grad = jnp.where(member_live[:, :, None, None], whole_grad[member_ids], zero_half)
        block_grad = block_grad.reshape(capacity, block_most * unit_rows, right_cols)
        direction = jnp.einsum(
            "irc,ick->irk", panel_rows, block_grad, preferred_element_type=jnp.float32
        )
        stepped = point - direction
        updated = jnp.sign(stepped) * jnp.maximum(jnp.abs(stepped) - penalty, 0.0)
        updated = jnp.where(slot_live[:, None, None], updated, jnp.float32(0.0))
        previous, current = (current, updated)
    return (current, residual)


def solution(mesh):
    placed = (
        P("samp", "var"),
        P(("samp", "var"), None),
        P("var", "samp", None),
        P("var", "samp", None),
        P("var", "samp", None, None),
        P(),
        P(),
        P(),
    )
    return jax.shard_map(
        shards,
        mesh=mesh,
        in_specs=placed,
        out_specs=(P("var", "samp", None), P(("samp", "var"), None)),
        check_vma=False,
    )
```

profile of v0, /device:TPU:0, one launch (start us, length us, event | category | flops | bytes accessed | tf_op | source)
XLA Modules:
  0.0 374.6 jit_solution(17077146969779160908)
XLA Ops:
  7.2 0.7 fusion.9
  8.0 0.7 broadcast_compare_fusion
  10.5 0.7 fusion.10
  11.8 0.8 select_reduce_fusion
  12.8 0.7 iota_subtract_fusion
  13.9 1.3 fusion.6
  15.9 4.6 %collective-permute-start = (bf16[4,64,128]{2,1,0:T(8,128)(2,1)S(1)}, bf16[4,64,128]{2,1,0:T(8,128)(2,1)S(1)}, u32[]{:S(2)}, u32[]{:S(2)}) collective-permute-start(bf16[4,64,128]{2,1,0:T(8,128)(2,1)S(1)} %get-tuple-element.27), channel_id=1, source_target_pairs={{1,0},{2,1},{3,2},{4,3},{5,4},{6,5},{7,6},{0,7},{9,8},{10,9},{11,1... | collective-permute-start | bytes 196616 | tf_op jit(solution)/shard_map/ppermute | solution.py:13
  20.5 3.3 collective-permute-start.1
  24.5 2.6 collective-permute-done.3
  27.7 11.3 %all-gather = bf16[8,256,128]{2,1,0:T(8,128)(2,1)S(1)} all-gather(bf16[8,64,128]{2,1,0:T(8,128)(2,1)S(1)} %gather_fusion.3), channel_id=2, replica_groups=mesh['samp'=4,'var'=8] {'samp'}, dimensions={1}, use_global_device_ids=true | all-gather | bytes 655360 | tf_op jit(solution)/shard_map/all_gather | solution.py:104
  39.0 7.4 %fusion.3 = f32[2048,128]{0,1:T(8,128)} fusion(bf16[2048,128]{1,0:T(8,128)(2,1)S(1)} %bitcast.106, bf16[2048,2048]{1,0:T(8,128)(2,1)} %param.8), kind=kOutput, calls=%fused_computation.21 | convolution fusion | flops 1074003968 | bytes 9961472 | tf_op jit(solution)/shard_map/dot_general | solution.py:107
  46.8 32.6 %reduce-scatter.3.cloned.1.call-done = f32[256,128]{0,1:T(8,128)} async-done(((f32[2048,128]{0,1:T(8,128)}), f32[256,128]{0,1:T(8,128)}) %reduce-scatter.3.cloned.1.call-update) | async-done | bytes 131088 | tf_op jit(solution)/shard_map/reduce_scatter | solution.py:106
  79.4 0.9 subtract_convert_fusion
  80.3 14.9 %all_gather.19 = bf16[2048,128]{0,1:T(8,128)(2,1)S(1)} all-gather(bf16[256,128]{0,1:T(8,128)(2,1)S(1)} %subtract_convert_fusion), channel_id=1, replica_groups=mesh['samp'=4,'var'=8] {'var'}, dimensions={0}, use_global_device_ids=true | all-gather | bytes 589824 | tf_op jit(solution)/shard_map/all_gather | solution.py:113
  95.3 4.7 %fusion.2 = f32[2048,128]{0,1:T(8,128)S(1)} fusion(bf16[2048,128]{0,1:T(8,128)(2,1)S(1)} %all_gather.19, bf16[2048,2048]{1,0:T(8,128)(2,1)} %param.8), kind=kOutput, calls=%fused_computation.19 | convolution fusion | flops 1074003968 | bytes 9961472 | tf_op jit(solution)/shard_map/dot_general | solution.py:115
  100.3 41.9 %all-reduce.2 = bf16[8,4,64,128]{3,2,1,0:T(8,128)(2,1)S(1)} all-reduce(f32[8,4,64,128]{3,2,1,0:T(8,128)S(1)} %bitcast.104), channel_id=1, replica_groups=mesh['samp'=4,'var'=8] {'samp'}, use_global_device_ids=true, to_apply=%region_12.13 | all-reduce | flops 262144 | bytes 1572864 | tf_op jit(solution)/shard_map/psum | solution.py:121
  143.1 0.7 collective-permute-start.7
  143.8 3.1 collective-permute-start.6
  146.9 1.7 collective-permute-done.4
  148.6 4.5 %collective-permute-done.7 = bf16[4,64,128]{2,1,0:T(8,128)(2,1)S(1)} collective-permute-done((bf16[4,64,128]{2,1,0:T(8,128)(2,1)S(1)}, bf16[4,64,128]{2,1,0:T(8,128)(2,1)S(1)}, u32[]{:S(2)}, u32[]{:S(2)}) %collective-permute-start.7) | collective-permute-done | bytes 65568 | tf_op jit(solution)/shard_map/ppermute | solution.py:13
  153.8 0.8 bitcast_select_fusion.3
  155.1 3.2 reshape.362
  158.3 20.1 %all-gather.5.cloned.1.call-done = bf16[16,4,64,128]{3,2,1,0:T(8,128)(2,1)} async-done(((bf16[16,1,64,128]{3,2,1,0:T(8,128)(2,1)}), bf16[16,4,64,128]{3,2,1,0:T(8,128)(2,1)}) %all-gather.5.cloned.1.call-update) | async-done | bytes 1048592 | tf_op jit(solution)/shard_map/all_gather | solution.py:132
  178.5 4.2 %gather_fusion.6 = bf16[64,256,128]{2,1,0:T(8,128)(2,1)} fusion(bf16[16,256,128]{2,1,0:T(8,128)(2,1)} %bitcast.100, s32[1024]{0:T(1024)S(1)} %pad_clamp_fusion), kind=kCustom, calls=%fused_computation.6 | custom fusion | bytes 8388864 | tf_op jit(solution)/shard_map/gather | solution.py:134
  182.7 6.2 %bitcast_select_fusion.1 = bf16[16,1024,128]{2,1,0:T(8,128)(2,1)S(1)} fusion(pred[16,1024]{1,0:T(8,128)(4,1)S(1)} %bitcast.112, bf16[16,1024,128]{2,1,0:T(8,128)(2,1)} %bitcast.103), kind=kLoop, calls=%fused_computation.13 | loop fusion | flops 2097152 | bytes 8404992 | tf_op jit(solution)/shard_map/jit(_where)/select_n | solution.py:134
  188.9 1.8 fusion.36
  191.5 2.7 collective-permute-start.8
  194.3 3.3 collective-permute-start.9
  197.6 3.1 collective-permute-done.11
  201.3 11.5 %all-gather.1 = bf16[8,256,128]{2,1,0:T(8,128)(2,1)S(1)} all-gather(bf16[8,64,128]{2,1,0:T(8,128)(2,1)S(1)} %gather_fusion.8), channel_id=3, replica_groups=mesh['samp'=4,'var'=8] {'samp'}, dimensions={1}, use_global_device_ids=true | all-gather | bytes 655360 | tf_op jit(solution)/shard_map/all_gather | solution.py:104
  212.9 7.3 %fusion.1 = f32[2048,128]{0,1:T(8,128)} fusion(bf16[2048,128]{1,0:T(8,128)(2,1)S(1)} %bitcast.107, bf16[2048,2048]{1,0:T(8,128)(2,1)} %param.8), kind=kOutput, calls=%fused_computation.17 | convolution fusion | flops 1074003968 | bytes 9961472 | tf_op jit(solution)/shard_map/dot_general | solution.py:107
  220.2 33.1 %reduce-scatter.5.cloned.1.call-done = f32[256,128]{0,1:T(8,128)} async-done(((f32[2048,128]{0,1:T(8,128)}), f32[256,128]{0,1:T(8,128)}) %reduce-scatter.5.cloned.1.call-update) | async-done | bytes 131088 | tf_op jit(solution)/shard_map/reduce_scatter | solution.py:106
  253.3 0.9 fusion.31
  254.2 14.9 %all_gather.22 = bf16[2048,128]{0,1:T(8,128)(2,1)S(1)} all-gather(bf16[256,128]{0,1:T(8,128)(2,1)S(1)} %get-tuple-element.13), channel_id=1, replica_groups=mesh['samp'=4,'var'=8] {'var'}, dimensions={0}, use_global_device_ids=true | all-gather | bytes 589824 | tf_op jit(solution)/shard_map/all_gather | solution.py:113
  269.2 5.7 %fusion = f32[2048,128]{0,1:T(8,128)} fusion(bf16[2048,128]{0,1:T(8,128)(2,1)S(1)} %all_gather.22, bf16[2048,2048]{1,0:T(8,128)(2,1)} %param.8), kind=kOutput, calls=%fused_computation.15 | convolution fusion | flops 1074003968 | bytes 9961472 | tf_op jit(solution)/shard_map/dot_general | solution.py:115
  274.9 1.5 copy.27
  276.4 42.3 %all-reduce.3 = bf16[8,4,64,128]{3,2,1,0:T(8,128)(2,1)} all-reduce(f32[8,4,64,128]{3,2,1,0:T(8,128)S(1)} %bitcast.105), channel_id=1, replica_groups=mesh['samp'=4,'var'=8] {'samp'}, use_global_device_ids=true, to_apply=%region_16.17 | all-reduce | flops 262144 | bytes 1572864 | tf_op jit(solution)/shard_map/psum | solution.py:121
  318.8 0.9 fusion.8
  320.5 0.7 collective-permute-start.15
  321.2 3.1 collective-permute-start.14
  324.3 1.8 collective-permute-done.12
  326.0 4.5 %collective-permute-done.15 = bf16[4,64,128]{2,1,0:T(8,128)(2,1)S(1)} collective-permute-done((bf16[4,64,128]{2,1,0:T(8,128)(2,1)S(1)}, bf16[4,64,128]{2,1,0:T(8,128)(2,1)S(1)}, u32[]{:S(2)}, u32[]{:S(2)}) %collective-permute-start.15) | collective-permute-done | bytes 65568 | tf_op jit(solution)/shard_map/ppermute | solution.py:13
  331.3 0.8 bitcast_select_fusion.2
  332.1 0.8 copy.28
  332.8 23.1 %all-gather.7.cloned.1.call-done = bf16[16,4,64,128]{3,2,1,0:T(8,128)(2,1)} async-done(((bf16[16,1,64,128]{3,2,1,0:T(8,128)(2,1)}), bf16[16,4,64,128]{3,2,1,0:T(8,128)(2,1)}) %all-gather.7.cloned.1.call-update) | async-done | bytes 1048592 | tf_op jit(solution)/shard_map/all_gather | solution.py:132
  355.9 4.2 %gather_fusion.11 = bf16[64,256,128]{2,1,0:T(8,128)(2,1)} fusion(bf16[16,256,128]{2,1,0:T(8,128)(2,1)} %bitcast.101, s32[1024]{0:T(1024)S(1)} %pad_clamp_fusion), kind=kCustom, calls=%fused_computation.11 | custom fusion | bytes 8388864 | tf_op jit(solution)/shard_map/gather | solution.py:134
  360.1 6.1 %bitcast_select_fusion = bf16[16,1024,128]{2,1,0:T(8,128)(2,1)S(1)} fusion(pred[16,1024]{1,0:T(8,128)(4,1)S(1)} %bitcast.113, bf16[16,1024,128]{2,1,0:T(8,128)(2,1)} %bitcast.102), kind=kLoop, calls=%fused_computation.12 | loop fusion | flops 2097152 | bytes 8404992 | tf_op jit(solution)/shard_map/jit(_where)/select_n | solution.py:134
  366.3 1.8 multiply_select_fusion
  (94 shorter events, 10.6 us)
Async XLA Ops:
  7.2 72.2 %reduce-scatter.3.cloned.1.call-start = ((), (), s32[]{:S(2)}) async-start(), calls=%async_computation.2 | async-start | bytes 1179648 | tf_op jit(solution)/shard_map/reduce_scatter | solution.py:106
  15.9 8.6 %collective-permute-start = (bf16[4,64,128]{2,1,0:T(8,128)(2,1)S(1)}, bf16[4,64,128]{2,1,0:T(8,128)(2,1)S(1)}, u32[]{:S(2)}, u32[]{:S(2)}) collective-permute-start(bf16[4,64,128]{2,1,0:T(8,128)(2,1)S(1)} %get-tuple-element.27), channel_id=1, source_target_pairs={{1,0},{2,1},{3,2},{4,3},{5,4},{6,5},{7,6},{0,7},{9,8},{10,9},{11,1... | collective-permute-start | bytes 196616 | tf_op jit(solution)/shard_map/ppermute | solution.py:13
  20.5 6.6 %collective-permute-start.3 = (bf16[4,64,128]{2,1,0:T(8,128)(2,1)S(1)}, bf16[4,64,128]{2,1,0:T(8,128)(2,1)S(1)}, u32[]{:S(2)}, u32[]{:S(2)}) collective-permute-start(bf16[4,64,128]{2,1,0:T(8,128)(2,1)S(1)} %get-tuple-element.28), channel_id=1, source_target_pairs={{4,0},{5,1},{6,2},{7,3},{0,4},{1,5},{2,6},{3,7},{12,8},{13,9},{14,... | collective-permute-start | bytes 196616 | tf_op jit(solution)/shard_map/ppermute | solution.py:13
  20.5 6.6 %collective-permute-start.2 = (bf16[4,64,128]{2,1,0:T(8,128)(2,1)S(1)}, bf16[4,64,128]{2,1,0:T(8,128)(2,1)S(1)}, u32[]{:S(2)}, u32[]{:S(2)}) collective-permute-start(bf16[4,64,128]{2,1,0:T(8,128)(2,1)S(1)} %get-tuple-element.29), channel_id=1, source_target_pairs={{3,0},{4,1},{5,2},{6,3},{7,4},{0,5},{1,6},{2,7},{11,8},{12,9},{13,... | collective-permute-start | bytes 196616 | tf_op jit(solution)/shard_map/ppermute | solution.py:13
  20.5 6.6 %collective-permute-start.1 = (bf16[4,64,128]{2,1,0:T(8,128)(2,1)S(1)}, bf16[4,64,128]{2,1,0:T(8,128)(2,1)S(1)}, u32[]{:S(2)}, u32[]{:S(2)}) collective-permute-start(bf16[4,64,128]{2,1,0:T(8,128)(2,1)S(1)} %get-tuple-element.30), channel_id=1, source_target_pairs={{2,0},{3,1},{4,2},{5,3},{6,4},{7,5},{0,6},{1,7},{10,8},{11,9},{12,... | collective-permute-start | bytes 196616 | tf_op jit(solution)/shard_map/ppermute | solution.py:13
  39.0 7.4 %copy-start.3 = (f32[256,128]{1,0:T(8,128)S(1)}, f32[256,128]{1,0:T(8,128)}, u32[]{:S(2)}) copy-start(f32[256,128]{1,0:T(8,128)} %param.9) | copy-start | bytes 393220
  46.4 132.1 %all-gather.5.cloned.1.call-start = ((), (), s32[]{:S(2)}) async-start(), calls=%async_computation.3 | async-start | bytes 1310720 | tf_op jit(solution)/shard_map/all_gather | solution.py:132
  143.0 5.6 %collective-permute-start.4 = (bf16[4,64,128]{2,1,0:T(8,128)(2,1)S(1)}, bf16[4,64,128]{2,1,0:T(8,128)(2,1)S(1)}, u32[]{:S(2)}, u32[]{:S(2)}) collective-permute-start(bf16[4,64,128]{2,1,0:T(8,128)(2,1)S(1)} %get-tuple-element.23), channel_id=1, source_target_pairs={{7,0},{0,1},{1,2},{2,3},{3,4},{4,5},{5,6},{6,7},{15,8},{8,9},{9,10... | collective-permute-start | bytes 196616 | tf_op jit(solution)/shard_map/ppermute | solution.py:13
  143.1 10.1 %collective-permute-start.7 = (bf16[4,64,128]{2,1,0:T(8,128)(2,1)S(1)}, bf16[4,64,128]{2,1,0:T(8,128)(2,1)S(1)}, u32[]{:S(2)}, u32[]{:S(2)}) collective-permute-start(bf16[4,64,128]{2,1,0:T(8,128)(2,1)S(1)} %get-tuple-element.24), channel_id=1, source_target_pairs={{4,0},{5,1},{6,2},{7,3},{0,4},{1,5},{2,6},{3,7},{12,8},{13,9},{14,... | collective-permute-start | bytes 196616 | tf_op jit(solution)/shard_map/ppermute | solution.py:13
  143.8 9.4 %collective-permute-start.6 = (bf16[4,64,128]{2,1,0:T(8,128)(2,1)S(1)}, bf16[4,64,128]{2,1,0:T(8,128)(2,1)S(1)}, u32[]{:S(2)}, u32[]{:S(2)}) collective-permute-start(bf16[4,64,128]{2,1,0:T(8,128)(2,1)S(1)} %get-tuple-element.25), channel_id=1, source_target_pairs={{5,0},{6,1},{7,2},{0,3},{1,4},{2,5},{3,6},{4,7},{13,8},{14,9},{15,... | collective-permute-start | bytes 196616 | tf_op jit(solution)/shard_map/ppermute | solution.py:13
  146.9 6.3 %collective-permute-start.5 = (bf16[4,64,128]{2,1,0:T(8,128)(2,1)S(1)}, bf16[4,64,128]{2,1,0:T(8,128)(2,1)S(1)}, u32[]{:S(2)}, u32[]{:S(2)}) collective-permute-start(bf16[4,64,128]{2,1,0:T(8,128)(2,1)S(1)} %get-tuple-element.26), channel_id=1, source_target_pairs={{6,0},{7,1},{0,2},{1,3},{2,4},{3,5},{4,6},{5,7},{14,8},{15,9},{8,1... | collective-permute-start | bytes 196616 | tf_op jit(solution)/shard_map/ppermute | solution.py:13
  154.7 98.7 %reduce-scatter.5.cloned.1.call-start = ((), (), s32[]{:S(2)}) async-start(), calls=%async_computation.4 | async-start | bytes 1179648 | tf_op jit(solution)/shard_map/reduce_scatter | solution.py:106
  182.7 6.2 %copy-start = (f32[16,64,128]{2,1,0:T(8,128)S(1)}, f32[16,64,128]{2,1,0:T(8,128)}, u32[]{:S(2)}) copy-start(f32[16,64,128]{2,1,0:T(8,128)} %param.10) | copy-start | bytes 1572868
  182.7 6.2 %copy-start.1 = (f32[16,64,128]{2,1,0:T(8,128)S(1)}, f32[16,64,128]{2,1,0:T(8,128)}, u32[]{:S(2)}) copy-start(f32[16,64,128]{2,1,0:T(8,128)} %param.11) | copy-start | bytes 1572868
  182.7 6.2 %copy-start.4 = (f32[128]{0:T(128)S(1)}, f32[128]{0:T(128)}, u32[]{:S(2)}) copy-start(f32[128]{0:T(128)} %param.13) | copy-start | bytes 1540
  191.5 6.1 %collective-permute-start.8 = (bf16[4,64,128]{2,1,0:T(8,128)(2,1)S(1)}, bf16[4,64,128]{2,1,0:T(8,128)(2,1)S(1)}, u32[]{:S(2)}, u32[]{:S(2)}) collective-permute-start(bf16[4,64,128]{2,1,0:T(8,128)(2,1)S(1)} %get-tuple-element.19), channel_id=1, source_target_pairs={{1,0},{2,1},{3,2},{4,3},{5,4},{6,5},{7,6},{0,7},{9,8},{10,9},{11,1... | collective-permute-start | bytes 196616 | tf_op jit(solution)/shard_map/ppermute | solution.py:13
  194.1 6.6 %collective-permute-start.11 = (bf16[4,64,128]{2,1,0:T(8,128)(2,1)S(1)}, bf16[4,64,128]{2,1,0:T(8,128)(2,1)S(1)}, u32[]{:S(2)}, u32[]{:S(2)}) collective-permute-start(bf16[4,64,128]{2,1,0:T(8,128)(2,1)S(1)} %get-tuple-element.20), channel_id=1, source_target_pairs={{4,0},{5,1},{6,2},{7,3},{0,4},{1,5},{2,6},{3,7},{12,8},{13,9},{14,... | collective-permute-start | bytes 196616 | tf_op jit(solution)/shard_map/ppermute | solution.py:13
  194.1 6.6 %collective-permute-start.10 = (bf16[4,64,128]{2,1,0:T(8,128)(2,1)S(1)}, bf16[4,64,128]{2,1,0:T(8,128)(2,1)S(1)}, u32[]{:S(2)}, u32[]{:S(2)}) collective-permute-start(bf16[4,64,128]{2,1,0:T(8,128)(2,1)S(1)} %get-tuple-element.21), channel_id=1, source_target_pairs={{3,0},{4,1},{5,2},{6,3},{7,4},{0,5},{1,6},{2,7},{11,8},{12,9},{13,... | collective-permute-start | bytes 196616 | tf_op jit(solution)/shard_map/ppermute | solution.py:13
  194.3 6.4 %collective-permute-start.9 = (bf16[4,64,128]{2,1,0:T(8,128)(2,1)S(1)}, bf16[4,64,128]{2,1,0:T(8,128)(2,1)S(1)}, u32[]{:S(2)}, u32[]{:S(2)}) collective-permute-start(bf16[4,64,128]{2,1,0:T(8,128)(2,1)S(1)} %get-tuple-element.22), channel_id=1, source_target_pairs={{2,0},{3,1},{4,2},{5,3},{6,4},{7,5},{0,6},{1,7},{10,8},{11,9},{12,... | collective-permute-start | bytes 196616 | tf_op jit(solution)/shard_map/ppermute | solution.py:13
  220.2 135.7 %all-gather.7.cloned.1.call-start = ((), (), s32[]{:S(2)}) async-start(), calls=%async_computation.5 | async-start | bytes 1310720 | tf_op jit(solution)/shard_map/all_gather | solution.py:132
  320.4 5.6 %collective-permute-start.12 = (bf16[4,64,128]{2,1,0:T(8,128)(2,1)S(1)}, bf16[4,64,128]{2,1,0:T(8,128)(2,1)S(1)}, u32[]{:S(2)}, u32[]{:S(2)}) collective-permute-start(bf16[4,64,128]{2,1,0:T(8,128)(2,1)S(1)} %get-tuple-element.15), channel_id=1, source_target_pairs={{7,0},{0,1},{1,2},{2,3},{3,4},{4,5},{5,6},{6,7},{15,8},{8,9},{9,10... | collective-permute-start | bytes 196616 | tf_op jit(solution)/shard_map/ppermute | solution.py:13
  320.5 10.1 %collective-permute-start.15 = (bf16[4,64,128]{2,1,0:T(8,128)(2,1)S(1)}, bf16[4,64,128]{2,1,0:T(8,128)(2,1)S(1)}, u32[]{:S(2)}, u32[]{:S(2)}) collective-permute-start(bf16[4,64,128]{2,1,0:T(8,128)(2,1)S(1)} %get-tuple-element.16), channel_id=1, source_target_pairs={{4,0},{5,1},{6,2},{7,3},{0,4},{1,5},{2,6},{3,7},{12,8},{13,9},{14,... | collective-permute-start | bytes 196616 | tf_op jit(solution)/shard_map/ppermute | solution.py:13
  321.2 9.4 %collective-permute-start.14 = (bf16[4,64,128]{2,1,0:T(8,128)(2,1)S(1)}, bf16[4,64,128]{2,1,0:T(8,128)(2,1)S(1)}, u32[]{:S(2)}, u32[]{:S(2)}) collective-permute-start(bf16[4,64,128]{2,1,0:T(8,128)(2,1)S(1)} %get-tuple-element.17), channel_id=1, source_target_pairs={{5,0},{6,1},{7,2},{0,3},{1,4},{2,5},{3,6},{4,7},{13,8},{14,9},{15,... | collective-permute-start | bytes 196616 | tf_op jit(solution)/shard_map/ppermute | solution.py:13
  324.3 6.3 %collective-permute-start.13 = (bf16[4,64,128]{2,1,0:T(8,128)(2,1)S(1)}, bf16[4,64,128]{2,1,0:T(8,128)(2,1)S(1)}, u32[]{:S(2)}, u32[]{:S(2)}) collective-permute-start(bf16[4,64,128]{2,1,0:T(8,128)(2,1)S(1)} %get-tuple-element.18), channel_id=1, source_target_pairs={{6,0},{7,1},{0,2},{1,3},{2,4},{3,5},{4,6},{5,7},{14,8},{15,9},{8,1... | collective-permute-start | bytes 196616 | tf_op jit(solution)/shard_map/ppermute | solution.py:13
  360.1 6.1 %copy-start.2 = (f32[16,64,128]{2,1,0:T(8,128)S(1)}, f32[16,64,128]{2,1,0:T(8,128)}, u32[]{:S(2)}) copy-start(f32[16,64,128]{2,1,0:T(8,128)} %get-tuple-element.36) | copy-start | bytes 1572868
Sparse Core Ops, SparseCore 0:
  46.5 32.8 reduce-scatter.2
  154.8 23.6 all-gather.4
  220.3 32.9 reduce-scatter.4
  332.2 23.6 all-gather.6
where the time goes:
time: 375 us
  blocking collectives  137 us (37%)
  waiting for transfers between devices  127 us (34%)
  matrix products  28.7 us (8%)
  other arithmetic  23.6 us (6%)
  starting transfers between devices  21.9 us (6%)
  local copies, waits for them, and re-layouts  21.9 us (6%)
  between operations  14.2 us (4%)
    psum x2, blocking collectives, shards(): grad_sum = lax.psum(shaped, 'samp')  84.2 us
    reduce_scatter x2, waiting for transfers between devices, shards(): lax.psum_scatter(jnp.dot(dosage, values, preferred_element_type=jnp.float...  65.7 us
    all_gather x2, waiting for transfers between devices, shards(): gathered = lax.all_gather(held_rows[:, None], 'samp', axis=1, tiled=True)  43.2 us
    all_gather x2, blocking collectives, shards(): lax.all_gather(residual.astype(jnp.bfloat16), 'var', axis=0, tiled=True)  29.9 us
    all_gather x2, blocking collectives, shards(): lax.all_gather(local_rows[:, None], 'samp', axis=1, tiled=True)  22.8 us
    ppermute x16, starting transfers between devices, shifted(): return lax.ppermute(block, axis, route)  21.8 us
    ppermute x16, waiting for transfers between devices, shifted(): return lax.ppermute(block, axis, route)  18.3 us
    dot_general x2, matrix products, shards(): jnp.dot(dosage, values, preferred_element_type=jnp.float32) * inv_scale  14.7 us
  transfers between devices with their start and end apart: 20, of which 12 were waited for; matrix products, arithmetic and copies ran while one was open for 1% of the time, Pallas kernels for 0%

commit v1 on v0

--- a/solution.py
+++ b/solution.py
@@ -118,7 +118,8 @@
             * grad_scale
         )
         shaped = partial_grad.reshape(per_device, quarters, quarter_rows, right_cols)
-        grad_sum = lax.psum(shaped, "samp")
+        terms = lax.all_gather(shaped, "samp", axis=0, tiled=False)
+        grad_sum = terms.sum(axis=0)
         own_grad = lax.dynamic_index_in_dim(grad_sum, samp_index, 1, keepdims=False)
         outgoing = jnp.where(
             send_live[:, None, None], own_grad.astype(jnp.bfloat16)[send_unit], zero_half

time: 375 us -> 402 us (1.072)
  waiting for transfers between devices: 127 us -> 232 us
  blocking collectives: 137 us -> 52.7 us
  other arithmetic: 23.6 us -> 29 us
    all_gather x0 -> x2, waiting for transfers between devices: none -> 102 us  [shards(): terms = lax.all_gather(shaped, 'samp', axis=0, tiled=False)]
    psum x2 -> x0, blocking collectives: 84.2 us -> none  [shards(): grad_sum = lax.psum(shaped, 'samp')]
    reduce_sum x0 -> x2, other arithmetic: none -> 5.38 us  [shards(): grad_sum = terms.sum(axis=0)]
  transfers between devices with their start and end apart: 20 -> 22, of which waited for: 12 -> 14; matrix products, arithmetic and copies ran while one was open for 1% -> 1% of each run, Pallas kernels for 0% -> 0%
where the time goes in v1:
time: 402 us; the launch traced here: 401 us
  waiting for transfers between devices  232 us (58%)
  blocking collectives  52.7 us (13%)
  other arithmetic  29 us (7%)
  matrix products  27.7 us (7%)
  starting transfers between devices  23.2 us (6%)
  local copies, waits for them, and re-layouts  21.8 us (5%)
  between operations  14.5 us (4%)
    all_gather x2, waiting for transfers between devices, shards(): terms = lax.all_gather(shaped, 'samp', axis=0, tiled=False)  102 us
    reduce_scatter x2, waiting for transfers between devices, shards(): lax.psum_scatter(jnp.dot(dosage, values, preferred_element_type=jnp.float...  66 us
    all_gather x2, waiting for transfers between devices, shards(): gathered = lax.all_gather(held_rows[:, None], 'samp', axis=1, tiled=True)  44.8 us
    all_gather x2, blocking collectives, shards(): lax.all_gather(residual.astype(jnp.bfloat16), 'var', axis=0, tiled=True)  29.9 us
    ppermute x16, starting transfers between devices, shifted(): return lax.ppermute(block, axis, route)  23 us
    all_gather x2, blocking collectives, shards(): lax.all_gather(local_rows[:, None], 'samp', axis=1, tiled=True)  22.8 us
    ppermute x16, waiting for transfers between devices, shifted(): return lax.ppermute(block, axis, route)  19.9 us
    dot_general x2, matrix products, shards(): jnp.dot(dosage, values, preferred_element_type=jnp.float32) * inv_scale  14.7 us
  transfers between devices with their start and end apart: 22, of which 14 were waited for; matrix products, arithmetic and copies ran while one was open for 1% of the time, Pallas kernels for 0%

profile of v1, /device:TPU:0, one launch (start us, length us, event | category | flops | bytes accessed | tf_op | source)
XLA Modules:
  0.0 401.3 jit_solution(13274450160256288676)
XLA Ops:
  11.8 0.8 select_reduce_fusion
  13.9 1.3 fusion.6
  15.9 4.6 %collective-permute-start = (bf16[4,64,128]{2,1,0:T(8,128)(2,1)S(1)}, bf16[4,64,128]{2,1,0:T(8,128)(2,1)S(1)}, u32[]{:S(2)}, u32[]{:S(2)}) collective-permute-start(bf16[4,64,128]{2,1,0:T(8,128)(2,1)S(1)} %get-tuple-element.29), channel_id=1, source_target_pairs={{1,0},{2,1},{3,2},{4,3},{5,4},{6,5},{7,6},{0,7},{9,8},{10,9},{11,1... | collective-permute-start | bytes 196616 | tf_op jit(solution)/shard_map/ppermute | solution.py:13
  20.5 3.3 collective-permute-start.1
  24.5 2.6 collective-permute-done.3
  27.7 11.3 %all-gather = bf16[8,256,128]{2,1,0:T(8,128)(2,1)S(1)} all-gather(bf16[8,64,128]{2,1,0:T(8,128)(2,1)S(1)} %gather_fusion.3), channel_id=2, replica_groups=mesh['samp'=4,'var'=8] {'samp'}, dimensions={1}, use_global_device_ids=true | all-gather | bytes 655360 | tf_op jit(solution)/shard_map/all_gather | solution.py:104
  39.0 7.4 %fusion.3 = f32[2048,128]{0,1:T(8,128)} fusion(bf16[2048,128]{1,0:T(8,128)(2,1)S(1)} %bitcast.106, bf16[2048,2048]{1,0:T(8,128)(2,1)} %param.8), kind=kOutput, calls=%fused_computation.21 | convolution fusion | flops 1074003968 | bytes 9961472 | tf_op jit(solution)/shard_map/dot_general | solution.py:107
  46.6 32.8 %reduce-scatter.3.cloned.1.call-done = f32[256,128]{0,1:T(8,128)} async-done(((f32[2048,128]{0,1:T(8,128)}), f32[256,128]{0,1:T(8,128)}) %reduce-scatter.3.cloned.1.call-update) | async-done | bytes 131088 | tf_op jit(solution)/shard_map/reduce_scatter | solution.py:106
  79.4 0.9 subtract_convert_fusion
  80.3 14.9 %all_gather.25 = bf16[2048,128]{0,1:T(8,128)(2,1)S(1)} all-gather(bf16[256,128]{0,1:T(8,128)(2,1)S(1)} %subtract_convert_fusion), channel_id=1, replica_groups=mesh['samp'=4,'var'=8] {'var'}, dimensions={0}, use_global_device_ids=true | all-gather | bytes 589824 | tf_op jit(solution)/shard_map/all_gather | solution.py:113
  95.3 4.7 %fusion.2 = f32[2048,128]{0,1:T(8,128)S(1)} fusion(bf16[2048,128]{0,1:T(8,128)(2,1)S(1)} %all_gather.25, bf16[2048,2048]{1,0:T(8,128)(2,1)} %param.8), kind=kOutput, calls=%fused_computation.19 | convolution fusion | flops 1074003968 | bytes 9961472 | tf_op jit(solution)/shard_map/dot_general | solution.py:115
  100.0 1.3 copy.32
  101.6 50.7 %all-gather.7.cloned.1.call-done = f32[4,8,4,64,128]{4,3,2,1,0:T(8,128)} async-done(((f32[1,8,4,64,128]{4,3,2,1,0:T(8,128)}), f32[4,8,4,64,128]{4,3,2,1,0:T(8,128)}) %all-gather.7.cloned.1.call-update) | async-done | bytes 4194320 | tf_op jit(solution)/shard_map/all_gather | solution.py:121
  152.3 2.7 reduce_sum.93
  155.8 2.5 collective-permute-start.7
  158.3 1.3 collective-permute-start.6
  160.2 1.2 collective-permute-done.4
  161.4 4.9 %collective-permute-done.7 = bf16[4,64,128]{2,1,0:T(8,128)(2,1)S(1)} collective-permute-done((bf16[4,64,128]{2,1,0:T(8,128)(2,1)S(1)}, bf16[4,64,128]{2,1,0:T(8,128)(2,1)S(1)}, u32[]{:S(2)}, u32[]{:S(2)}) %collective-permute-start.7) | collective-permute-done | bytes 65568 | tf_op jit(solution)/shard_map/ppermute | solution.py:13
  166.3 1.0 collective-permute-done.6
  168.0 0.8 bitcast_select_fusion.3
  169.2 3.2 reshape.355
  172.5 20.9 %all-gather.9.cloned.1.call-done = bf16[16,4,64,128]{3,2,1,0:T(8,128)(2,1)} async-done(((bf16[16,1,64,128]{3,2,1,0:T(8,128)(2,1)}), bf16[16,4,64,128]{3,2,1,0:T(8,128)(2,1)}) %all-gather.9.cloned.1.call-update) | async-done | bytes 1048592 | tf_op jit(solution)/shard_map/all_gather | solution.py:133
  193.4 4.2 %gather_fusion.6 = bf16[64,256,128]{2,1,0:T(8,128)(2,1)} fusion(bf16[16,256,128]{2,1,0:T(8,128)(2,1)} %bitcast.100, s32[1024]{0:T(1024)S(1)} %pad_clamp_fusion), kind=kCustom, calls=%fused_computation.6 | custom fusion | bytes 8388864 | tf_op jit(solution)/shard_map/gather | solution.py:135
  197.7 6.2 %bitcast_select_fusion.1 = bf16[16,1024,128]{2,1,0:T(8,128)(2,1)S(1)} fusion(pred[16,1024]{1,0:T(8,128)(4,1)S(1)} %bitcast.112, bf16[16,1024,128]{2,1,0:T(8,128)(2,1)} %bitcast.103), kind=kLoop, calls=%fused_computation.13 | loop fusion | flops 2097152 | bytes 8404992 | tf_op jit(solution)/shard_map/jit(_where)/select_n | solution.py:135
  203.9 1.8 fusion.36
  206.4 2.7 collective-permute-start.8
  209.2 3.3 collective-permute-start.9
  212.6 3.1 collective-permute-done.11
  216.3 11.5 %all-gather.1 = bf16[8,256,128]{2,1,0:T(8,128)(2,1)S(1)} all-gather(bf16[8,64,128]{2,1,0:T(8,128)(2,1)S(1)} %gather_fusion.8), channel_id=3, replica_groups=mesh['samp'=4,'var'=8] {'samp'}, dimensions={1}, use_global_device_ids=true | all-gather | bytes 655360 | tf_op jit(solution)/shard_map/all_gather | solution.py:104
  227.8 7.3 %fusion.1 = f32[2048,128]{0,1:T(8,128)} fusion(bf16[2048,128]{1,0:T(8,128)(2,1)S(1)} %bitcast.107, bf16[2048,2048]{1,0:T(8,128)(2,1)} %param.8), kind=kOutput, calls=%fused_computation.17 | convolution fusion | flops 1074003968 | bytes 9961472 | tf_op jit(solution)/shard_map/dot_general | solution.py:107
  235.2 33.1 %reduce-scatter.5.cloned.1.call-done = f32[256,128]{0,1:T(8,128)} async-done(((f32[2048,128]{0,1:T(8,128)}), f32[256,128]{0,1:T(8,128)}) %reduce-scatter.5.cloned.1.call-update) | async-done | bytes 131088 | tf_op jit(solution)/shard_map/reduce_scatter | solution.py:106
  268.3 0.9 fusion.31
  269.2 14.9 %all_gather.29 = bf16[2048,128]{0,1:T(8,128)(2,1)S(1)} all-gather(bf16[256,128]{0,1:T(8,128)(2,1)S(1)} %get-tuple-element.15), channel_id=1, replica_groups=mesh['samp'=4,'var'=8] {'var'}, dimensions={0}, use_global_device_ids=true | all-gather | bytes 589824 | tf_op jit(solution)/shard_map/all_gather | solution.py:113
  284.2 4.7 %fusion = f32[2048,128]{0,1:T(8,128)S(1)} fusion(bf16[2048,128]{0,1:T(8,128)(2,1)S(1)} %all_gather.29, bf16[2048,2048]{1,0:T(8,128)(2,1)} %param.8), kind=kOutput, calls=%fused_computation.15 | convolution fusion | flops 1074003968 | bytes 9961472 | tf_op jit(solution)/shard_map/dot_general | solution.py:115
  288.9 1.3 copy.34
  290.3 50.9 %all-gather.11.cloned.1.call-done = f32[4,8,4,64,128]{4,3,2,1,0:T(8,128)} async-done(((f32[1,8,4,64,128]{4,3,2,1,0:T(8,128)}), f32[4,8,4,64,128]{4,3,2,1,0:T(8,128)}) %all-gather.11.cloned.1.call-update) | async-done | bytes 4194320 | tf_op jit(solution)/shard_map/all_gather | solution.py:121
  341.2 2.7 reduce_sum.98
  344.7 2.5 collective-permute-start.15
  347.2 1.3 collective-permute-start.14
  349.1 1.2 collective-permute-done.12
  350.3 4.9 %collective-permute-done.15 = bf16[4,64,128]{2,1,0:T(8,128)(2,1)S(1)} collective-permute-done((bf16[4,64,128]{2,1,0:T(8,128)(2,1)S(1)}, bf16[4,64,128]{2,1,0:T(8,128)(2,1)S(1)}, u32[]{:S(2)}, u32[]{:S(2)}) %collective-permute-start.15) | collective-permute-done | bytes 65568 | tf_op jit(solution)/shard_map/ppermute | solution.py:13
  355.2 1.0 collective-permute-done.14
  356.9 0.8 bitcast_select_fusion.2
  357.7 0.8 copy.35
  358.5 23.8 %all-gather.13.cloned.1.call-done = bf16[16,4,64,128]{3,2,1,0:T(8,128)(2,1)} async-done(((bf16[16,1,64,128]{3,2,1,0:T(8,128)(2,1)}), bf16[16,4,64,128]{3,2,1,0:T(8,128)(2,1)}) %all-gather.13.cloned.1.call-update) | async-done | bytes 1048592 | tf_op jit(solution)/shard_map/all_gather | solution.py:133
  382.3 4.2 %gather_fusion.11 = bf16[64,256,128]{2,1,0:T(8,128)(2,1)} fusion(bf16[16,256,128]{2,1,0:T(8,128)(2,1)} %bitcast.101, s32[1024]{0:T(1024)S(1)} %pad_clamp_fusion), kind=kCustom, calls=%fused_computation.11 | custom fusion | bytes 8388864 | tf_op jit(solution)/shard_map/gather | solution.py:135
  386.5 6.1 %bitcast_select_fusion = bf16[16,1024,128]{2,1,0:T(8,128)(2,1)S(1)} fusion(pred[16,1024]{1,0:T(8,128)(4,1)S(1)} %bitcast.113, bf16[16,1024,128]{2,1,0:T(8,128)(2,1)} %bitcast.102), kind=kLoop, calls=%fused_computation.12 | loop fusion | flops 2097152 | bytes 8404992 | tf_op jit(solution)/shard_map/jit(_where)/select_n | solution.py:135
  392.7 1.8 multiply_select_fusion
  (100 shorter events, 14.3 us)
Async XLA Ops:
  7.2 72.2 %reduce-scatter.3.cloned.1.call-start = ((), (), s32[]{:S(2)}) async-start(), calls=%async_computation.2 | async-start | bytes 1179648 | tf_op jit(solution)/shard_map/reduce_scatter | solution.py:106
  15.9 8.6 %collective-permute-start = (bf16[4,64,128]{2,1,0:T(8,128)(2,1)S(1)}, bf16[4,64,128]{2,1,0:T(8,128)(2,1)S(1)}, u32[]{:S(2)}, u32[]{:S(2)}) collective-permute-start(bf16[4,64,128]{2,1,0:T(8,128)(2,1)S(1)} %get-tuple-element.29), channel_id=1, source_target_pairs={{1,0},{2,1},{3,2},{4,3},{5,4},{6,5},{7,6},{0,7},{9,8},{10,9},{11,1... | collective-permute-start | bytes 196616 | tf_op jit(solution)/shard_map/ppermute | solution.py:13
  20.5 6.6 %collective-permute-start.3 = (bf16[4,64,128]{2,1,0:T(8,128)(2,1)S(1)}, bf16[4,64,128]{2,1,0:T(8,128)(2,1)S(1)}, u32[]{:S(2)}, u32[]{:S(2)}) collective-permute-start(bf16[4,64,128]{2,1,0:T(8,128)(2,1)S(1)} %get-tuple-element.30), channel_id=1, source_target_pairs={{4,0},{5,1},{6,2},{7,3},{0,4},{1,5},{2,6},{3,7},{12,8},{13,9},{14,... | collective-permute-start | bytes 196616 | tf_op jit(solution)/shard_map/ppermute | solution.py:13
  20.5 6.6 %collective-permute-start.2 = (bf16[4,64,128]{2,1,0:T(8,128)(2,1)S(1)}, bf16[4,64,128]{2,1,0:T(8,128)(2,1)S(1)}, u32[]{:S(2)}, u32[]{:S(2)}) collective-permute-start(bf16[4,64,128]{2,1,0:T(8,128)(2,1)S(1)} %get-tuple-element.31), channel_id=1, source_target_pairs={{3,0},{4,1},{5,2},{6,3},{7,4},{0,5},{1,6},{2,7},{11,8},{12,9},{13,... | collective-permute-start | bytes 196616 | tf_op jit(solution)/shard_map/ppermute | solution.py:13
  20.5 6.6 %collective-permute-start.1 = (bf16[4,64,128]{2,1,0:T(8,128)(2,1)S(1)}, bf16[4,64,128]{2,1,0:T(8,128)(2,1)S(1)}, u32[]{:S(2)}, u32[]{:S(2)}) collective-permute-start(bf16[4,64,128]{2,1,0:T(8,128)(2,1)S(1)} %get-tuple-element.32), channel_id=1, source_target_pairs={{2,0},{3,1},{4,2},{5,3},{6,4},{7,5},{0,6},{1,7},{10,8},{11,9},{12,... | collective-permute-start | bytes 196616 | tf_op jit(solution)/shard_map/ppermute | solution.py:13
  39.0 7.4 %copy-start.3 = (f32[256,128]{1,0:T(8,128)S(1)}, f32[256,128]{1,0:T(8,128)}, u32[]{:S(2)}) copy-start(f32[256,128]{1,0:T(8,128)} %param.9) | copy-start | bytes 393220
  46.4 105.9 %all-gather.7.cloned.1.call-start = ((), (), s32[]{:S(2)}) async-start(), calls=%async_computation.3 | async-start | bytes 5242880 | tf_op jit(solution)/shard_map/all_gather | solution.py:121
  101.3 92.1 %all-gather.9.cloned.1.call-start = ((), (), s32[]{:S(2)}) async-start(), calls=%async_computation.4 | async-start | bytes 1310720 | tf_op jit(solution)/shard_map/all_gather | solution.py:133
  155.7 5.7 %collective-permute-start.4 = (bf16[4,64,128]{2,1,0:T(8,128)(2,1)S(1)}, bf16[4,64,128]{2,1,0:T(8,128)(2,1)S(1)}, u32[]{:S(2)}, u32[]{:S(2)}) collective-permute-start(bf16[4,64,128]{2,1,0:T(8,128)(2,1)S(1)} %get-tuple-element.25), channel_id=1, source_target_pairs={{7,0},{0,1},{1,2},{2,3},{3,4},{4,5},{5,6},{6,7},{15,8},{8,9},{9,10... | collective-permute-start | bytes 196616 | tf_op jit(solution)/shard_map/ppermute | solution.py:13
  155.8 10.5 %collective-permute-start.7 = (bf16[4,64,128]{2,1,0:T(8,128)(2,1)S(1)}, bf16[4,64,128]{2,1,0:T(8,128)(2,1)S(1)}, u32[]{:S(2)}, u32[]{:S(2)}) collective-permute-start(bf16[4,64,128]{2,1,0:T(8,128)(2,1)S(1)} %get-tuple-element.26), channel_id=1, source_target_pairs={{4,0},{5,1},{6,2},{7,3},{0,4},{1,5},{2,6},{3,7},{12,8},{13,9},{14,... | collective-permute-start | bytes 196616 | tf_op jit(solution)/shard_map/ppermute | solution.py:13
  158.3 9.1 %collective-permute-start.6 = (bf16[4,64,128]{2,1,0:T(8,128)(2,1)S(1)}, bf16[4,64,128]{2,1,0:T(8,128)(2,1)S(1)}, u32[]{:S(2)}, u32[]{:S(2)}) collective-permute-start(bf16[4,64,128]{2,1,0:T(8,128)(2,1)S(1)} %get-tuple-element.27), channel_id=1, source_target_pairs={{5,0},{6,1},{7,2},{0,3},{1,4},{2,5},{3,6},{4,7},{13,8},{14,9},{15,... | collective-permute-start | bytes 196616 | tf_op jit(solution)/shard_map/ppermute | solution.py:13
  159.6 7.7 %collective-permute-start.5 = (bf16[4,64,128]{2,1,0:T(8,128)(2,1)S(1)}, bf16[4,64,128]{2,1,0:T(8,128)(2,1)S(1)}, u32[]{:S(2)}, u32[]{:S(2)}) collective-permute-start(bf16[4,64,128]{2,1,0:T(8,128)(2,1)S(1)} %get-tuple-element.28), channel_id=1, source_target_pairs={{6,0},{7,1},{0,2},{1,3},{2,4},{3,5},{4,6},{5,7},{14,8},{15,9},{8,1... | collective-permute-start | bytes 196616 | tf_op jit(solution)/shard_map/ppermute | solution.py:13
  168.8 99.5 %reduce-scatter.5.cloned.1.call-start = ((), (), s32[]{:S(2)}) async-start(), calls=%async_computation.5 | async-start | bytes 1179648 | tf_op jit(solution)/shard_map/reduce_scatter | solution.py:106
  197.7 6.2 %copy-start = (f32[16,64,128]{2,1,0:T(8,128)S(1)}, f32[16,64,128]{2,1,0:T(8,128)}, u32[]{:S(2)}) copy-start(f32[16,64,128]{2,1,0:T(8,128)} %param.10) | copy-start | bytes 1572868
  197.7 6.2 %copy-start.1 = (f32[16,64,128]{2,1,0:T(8,128)S(1)}, f32[16,64,128]{2,1,0:T(8,128)}, u32[]{:S(2)}) copy-start(f32[16,64,128]{2,1,0:T(8,128)} %param.11) | copy-start | bytes 1572868
  197.7 6.2 %copy-start.4 = (f32[128]{0:T(128)S(1)}, f32[128]{0:T(128)}, u32[]{:S(2)}) copy-start(f32[128]{0:T(128)} %param.13) | copy-start | bytes 1540
  206.4 6.2 %collective-permute-start.8 = (bf16[4,64,128]{2,1,0:T(8,128)(2,1)S(1)}, bf16[4,64,128]{2,1,0:T(8,128)(2,1)S(1)}, u32[]{:S(2)}, u32[]{:S(2)}) collective-permute-start(bf16[4,64,128]{2,1,0:T(8,128)(2,1)S(1)} %get-tuple-element.21), channel_id=1, source_target_pairs={{1,0},{2,1},{3,2},{4,3},{5,4},{6,5},{7,6},{0,7},{9,8},{10,9},{11,1... | collective-permute-start | bytes 196616 | tf_op jit(solution)/shard_map/ppermute | solution.py:13
  209.1 6.6 %collective-permute-start.11 = (bf16[4,64,128]{2,1,0:T(8,128)(2,1)S(1)}, bf16[4,64,128]{2,1,0:T(8,128)(2,1)S(1)}, u32[]{:S(2)}, u32[]{:S(2)}) collective-permute-start(bf16[4,64,128]{2,1,0:T(8,128)(2,1)S(1)} %get-tuple-element.22), channel_id=1, source_target_pairs={{4,0},{5,1},{6,2},{7,3},{0,4},{1,5},{2,6},{3,7},{12,8},{13,9},{14,... | collective-permute-start | bytes 196616 | tf_op jit(solution)/shard_map/ppermute | solution.py:13
  209.1 6.6 %collective-permute-start.10 = (bf16[4,64,128]{2,1,0:T(8,128)(2,1)S(1)}, bf16[4,64,128]{2,1,0:T(8,128)(2,1)S(1)}, u32[]{:S(2)}, u32[]{:S(2)}) collective-permute-start(bf16[4,64,128]{2,1,0:T(8,128)(2,1)S(1)} %get-tuple-element.23), channel_id=1, source_target_pairs={{3,0},{4,1},{5,2},{6,3},{7,4},{0,5},{1,6},{2,7},{11,8},{12,9},{13,... | collective-permute-start | bytes 196616 | tf_op jit(solution)/shard_map/ppermute | solution.py:13
  209.2 6.4 %collective-permute-start.9 = (bf16[4,64,128]{2,1,0:T(8,128)(2,1)S(1)}, bf16[4,64,128]{2,1,0:T(8,128)(2,1)S(1)}, u32[]{:S(2)}, u32[]{:S(2)}) collective-permute-start(bf16[4,64,128]{2,1,0:T(8,128)(2,1)S(1)} %get-tuple-element.24), channel_id=1, source_target_pairs={{2,0},{3,1},{4,2},{5,3},{6,4},{7,5},{0,6},{1,7},{10,8},{11,9},{12,... | collective-permute-start | bytes 196616 | tf_op jit(solution)/shard_map/ppermute | solution.py:13
  235.1 106.0 %all-gather.11.cloned.1.call-start = ((), (), s32[]{:S(2)}) async-start(), calls=%async_computation.6 | async-start | bytes 5242880 | tf_op jit(solution)/shard_map/all_gather | solution.py:121
  290.2 92.1 %all-gather.13.cloned.1.call-start = ((), (), s32[]{:S(2)}) async-start(), calls=%async_computation.7 | async-start | bytes 1310720 | tf_op jit(solution)/shard_map/all_gather | solution.py:133
  344.6 5.7 %collective-permute-start.12 = (bf16[4,64,128]{2,1,0:T(8,128)(2,1)S(1)}, bf16[4,64,128]{2,1,0:T(8,128)(2,1)S(1)}, u32[]{:S(2)}, u32[]{:S(2)}) collective-permute-start(bf16[4,64,128]{2,1,0:T(8,128)(2,1)S(1)} %get-tuple-element.17), channel_id=1, source_target_pairs={{7,0},{0,1},{1,2},{2,3},{3,4},{4,5},{5,6},{6,7},{15,8},{8,9},{9,10... | collective-permute-start | bytes 196616 | tf_op jit(solution)/shard_map/ppermute | solution.py:13
  344.7 10.5 %collective-permute-start.15 = (bf16[4,64,128]{2,1,0:T(8,128)(2,1)S(1)}, bf16[4,64,128]{2,1,0:T(8,128)(2,1)S(1)}, u32[]{:S(2)}, u32[]{:S(2)}) collective-permute-start(bf16[4,64,128]{2,1,0:T(8,128)(2,1)S(1)} %get-tuple-element.18), channel_id=1, source_target_pairs={{4,0},{5,1},{6,2},{7,3},{0,4},{1,5},{2,6},{3,7},{12,8},{13,9},{14,... | collective-permute-start | bytes 196616 | tf_op jit(solution)/shard_map/ppermute | solution.py:13
  347.2 9.1 %collective-permute-start.14 = (bf16[4,64,128]{2,1,0:T(8,128)(2,1)S(1)}, bf16[4,64,128]{2,1,0:T(8,128)(2,1)S(1)}, u32[]{:S(2)}, u32[]{:S(2)}) collective-permute-start(bf16[4,64,128]{2,1,0:T(8,128)(2,1)S(1)} %get-tuple-element.19), channel_id=1, source_target_pairs={{5,0},{6,1},{7,2},{0,3},{1,4},{2,5},{3,6},{4,7},{13,8},{14,9},{15,... | collective-permute-start | bytes 196616 | tf_op jit(solution)/shard_map/ppermute | solution.py:13
  348.5 7.7 %collective-permute-start.13 = (bf16[4,64,128]{2,1,0:T(8,128)(2,1)S(1)}, bf16[4,64,128]{2,1,0:T(8,128)(2,1)S(1)}, u32[]{:S(2)}, u32[]{:S(2)}) collective-permute-start(bf16[4,64,128]{2,1,0:T(8,128)(2,1)S(1)} %get-tuple-element.20), channel_id=1, source_target_pairs={{6,0},{7,1},{0,2},{1,3},{2,4},{3,5},{4,6},{5,7},{14,8},{15,9},{8,1... | collective-permute-start | bytes 196616 | tf_op jit(solution)/shard_map/ppermute | solution.py:13
  386.5 6.1 %copy-start.2 = (f32[16,64,128]{2,1,0:T(8,128)S(1)}, f32[16,64,128]{2,1,0:T(8,128)}, u32[]{:S(2)}) copy-start(f32[16,64,128]{2,1,0:T(8,128)} %get-tuple-element.38) | copy-start | bytes 1572868
Sparse Core Ops, SparseCore 0:
  46.5 32.8 reduce-scatter.2
  101.4 50.8 all-gather.6
  168.9 24.4 all-gather.8
  235.3 33.0 reduce-scatter.4
  290.3 50.7 all-gather.10
  357.8 24.4 all-gather.12
